TPU v7x, 32 devices: a whole 2x2x4 slice. The times are simulated.
32 devices in a mesh: gx: 8 (over y, x, core), gy: 4 (over z).
Axes of the slice: x: 2, y: 2, z: 4, core: 2. Of those that a mesh axis runs over, the one named last changes fastest.
Arguments:
- wind_u: float32 [96, 128, 1024], P('gy', 'gx'), may hold values from -6 to 6
- wind_v: float32 [96, 128, 1024], P('gy', 'gx'), may hold values from -6 to 6
- pressure: float32 [96, 128, 1024], P(None, 'gx', 'gy'), may hold values from -6 to 6
- vertical_w: float32 [96, 128, 1024], P(None, 'gx', 'gy'), may hold values from -6 to 6
- theta: float32 [96, 128, 1024], P(None, 'gx', 'gy'), may hold values from -6 to 6
- terrain: int32 [128, 1024], P('gx', 'gy'), may hold values from 0 to 3
- inverses: float32 [4, 192, 192], replicated, may hold values from -1 to 2, as said below
Outputs:
- wind_u_out: float32 [96, 128, 1024], P('gy', 'gx')
- wind_v_out: float32 [96, 128, 1024], P('gy', 'gx')
- pressure_out: float32 [96, 128, 1024], P(None, 'gx', 'gy')
- vertical_w_out: float32 [96, 128, 1024], P(None, 'gx', 'gy')
- theta_out: float32 [96, 128, 1024], P(None, 'gx', 'gy')
Inputs may be any that keep to these rules, and one draw needn't show every extreme that they name: inverses has a diagonal between 0.6 and 1.6 and off-diagonal entries of order 1 / sqrt(192).
All inputs are finite; a program needn't handle non-finite values.
Results may differ from a plain program's by a relative error of at most 0.00013.
Values sent between devices are 32-bit elements; how exact they have to be, the bound alone decides.
A program may use at most 192 MiB of HBM per device.

v0:
```python
import jax
import jax.numpy as jnp
from jax import lax
from jax.sharding import PartitionSpec as P

SUBSTEPS = 4


def from_behind(value, axis, steps):
    count = lax.axis_size(axis)
    leading, last = (max(0, -steps), min(count, count - steps))
    return lax.ppermute(value, axis, [(source, source + steps) for source in range(leading, last)])


def column_update(pressure, vertical_w, theta, diverge, above, flat_terrain, inverses):
    levels = pressure.shape[0]
    columns_x = pressure.shape[1]
    columns_y = pressure.shape[2]
    below_p = jnp.pad(pressure, ((1, 0), (0, 0), (0, 0)))[:-1]
    rhs_w = vertical_w - 0.5 * (pressure - below_p)
    rhs_t = theta - 0.5 * diverge
    stacked = jnp.stack([rhs_w, rhs_t], axis=1).reshape(2 * levels, columns_x * columns_y)
    solved = jnp.zeros_like(stacked)
    for klass in range(inverses.shape[0]):
        product = jnp.dot(inverses[klass], stacked, precision=lax.Precision.HIGHEST)
        solved = solved + jnp.where(flat_terrain[None] == klass, product, 0.0)
    solved = solved.reshape(levels, 2, columns_x, columns_y)
    vertical_w = solved[:, 0] * above
    new_theta = solved[:, 1]
    pressure = pressure - 0.3 * diverge + 0.5 * (new_theta - theta)
    return (pressure, vertical_w, new_theta)


def per_device(wind_u, wind_v, pressure, vertical_w, theta, terrain, inverses):
    level_ids = lax.broadcasted_iota(jnp.int32, pressure.shape, 0)
    above = (level_ids >= terrain[None]).astype(jnp.float32)
    flat_terrain = terrain.reshape(-1)
    col_u, col_v = (
        lax.all_to_all(wind_u, "gy", split_axis=2, concat_axis=0, tiled=True),
        lax.all_to_all(wind_v, "gy", split_axis=2, concat_axis=0, tiled=True),
    )
    for step in range(SUBSTEPS):
        after_x = from_behind(pressure[:, :1], "gx", -1)
        after_y = from_behind(pressure[:, :, :1], "gy", -1)
        next_x = jnp.concatenate([pressure[:, 1:], after_x], axis=1)
        next_y = jnp.concatenate([pressure[:, :, 1:], after_y], axis=2)
        col_u = col_u - 0.5 * (next_x - pressure)
        col_v = col_v - 0.5 * (next_y - pressure)
        edge_u = from_behind(col_u[:, -1:], "gx", 1)
        edge_v = from_behind(col_v[:, :, -1:], "gy", 1)
        left_u = jnp.concatenate([edge_u, col_u[:, :-1]], axis=1)
        left_v = jnp.concatenate([edge_v, col_v[:, :, :-1]], axis=2)
        diverge = col_u - left_u + (col_v - left_v)
        pressure, vertical_w, theta = column_update(
            pressure, vertical_w, theta, diverge, above, flat_terrain, inverses
        )
    wind_u, wind_v = (
        lax.all_to_all(col_u, "gy", split_axis=0, concat_axis=2, tiled=True),
        lax.all_to_all(col_v, "gy", split_axis=0, concat_axis=2, tiled=True),
    )
    return (wind_u, wind_v, pressure, vertical_w, theta)


def solution(mesh):
    return jax.shard_map(
        per_device,
        mesh=mesh,
        in_specs=(
            P("gy", "gx", None),
            P("gy", "gx", None),
            P(None, "gx", "gy"),
            P(None, "gx", "gy"),
            P(None, "gx", "gy"),
            P("gx", "gy"),
            P(),
        ),
        out_specs=(
            P("gy", "gx", None),
            P("gy", "gx", None),
            P(None, "gx", "gy"),
            P(None, "gx", "gy"),
            P(None, "gx", "gy"),
        ),
        check_vma=False,
    )
```

profile of v0, /device:TPU:0, one launch (start us, length us, event | category | flops | bytes accessed | tf_op | source)
XLA Modules:
  0.0 396.8 jit_solution(9056120435132400761)
XLA Ops:
  0.6 7.4 %copy.140 = f32[24,16,1024]{0,1,2:T(8,128)} copy(f32[24,16,1024]{2,1,0:T(8,128)} %param.7) | data formatting | bytes 3145728 | tf_op args[0]
  8.0 9.2 %reshape.79 = f32[4,1,98304]{2,1,0:T(1,128)} reshape(f32[1024,16,24]{2,1,0:T(8,128)} %bitcast.209) | data formatting | bytes 3145728
  17.3 6.5 %all-to-all-start = ((f32[4,1,98304]{2,1,0:T(1,128)}), f32[4,1,98304]{2,1,0:T(1,128)S(1)}, u32[]{:S(2)}, u32[]{:S(2)}) async-start(f32[4,1,98304]{2,1,0:T(1,128)} %reshape.79), calls=%async_computation | async-start | bytes 3145728 | tf_op jit(solution)/shard_map/all_to_all | solution.py:39
  23.7 6.4 %copy.143 = f32[24,16,1024]{0,1,2:T(8,128)} copy(f32[24,16,1024]{2,1,0:T(8,128)S(1)} %copy-done.26) | data formatting | bytes 3145728 | tf_op args[1]
  30.2 9.2 %reshape.81 = f32[4,1,98304]{2,1,0:T(1,128)} reshape(f32[1024,16,24]{2,1,0:T(8,128)} %bitcast.210) | data formatting | bytes 3145728
  39.4 21.3 %all-to-all-done = f32[4,1,98304]{2,1,0:T(1,128)S(1)} async-done(((f32[4,1,98304]{2,1,0:T(1,128)}), f32[4,1,98304]{2,1,0:T(1,128)S(1)}, u32[]{:S(2)}, u32[]{:S(2)}) %all-to-all-start) | async-done | bytes 1572896 | tf_op jit(solution)/shard_map/all_to_all | solution.py:39
  61.8 4.4 %all-to-all-start.1 = ((f32[4,1,98304]{2,1,0:T(1,128)}), f32[4,1,98304]{2,1,0:T(1,128)}, u32[]{:S(2)}, u32[]{:S(2)}) async-start(f32[4,1,98304]{2,1,0:T(1,128)} %reshape.81), calls=%async_computation.1 | async-start | bytes 3145728 | tf_op jit(solution)/shard_map/all_to_all | solution.py:40
  72.9 12.4 %collective-permute-done.2 = f32[96,16,1]{0,1,2:T(8,128)S(1)} collective-permute-done((f32[96,16,1]{0,1,2:T(8,128)S(1)}, f32[96,16,1]{0,1,2:T(8,128)S(1)}, u32[]{:S(2)}, u32[]{:S(2)}) %collective-permute-start.2) | collective-permute-done | bytes 6176 | tf_op jit(solution)/shard_map/ppermute | solution.py:12
  87.1 6.2 %reduce.1 = f32[4,98304]{1,0:T(4,128)S(1)} reduce(f32[4,1,98304]{2,1,0:T(1,128)} %copy-done.24, f32[]{:T(128)} %broadcast.133), dimensions={1}, to_apply=%all_to_all.52.reduce_sub_computation | reduce | bytes 3145732 | tf_op jit(solution)/shard_map/all_to_all | solution.py:39
  93.3 9.6 %reshape.80 = f32[1024,16,24]{2,1,0:T(8,128)} reshape(f32[4,98304]{1,0:T(4,128)S(1)} %reduce.1) | data formatting | bytes 3145728
  102.8 6.0 %copy.176 = f32[24,16,4,256]{3,2,1,0:T(4,128)S(1)} copy(f32[24,16,4,256]{0,1,3,2:T(8,128)} %bitcast.207) | data formatting | bytes 3145728 | tf_op jit(solution)/shard_map/all_to_all | solution.py:39
  110.2 6.2 %reduce = f32[4,98304]{1,0:T(4,128)S(1)} reduce(f32[4,1,98304]{2,1,0:T(1,128)} %all-to-all-done.1, f32[]{:T(128)} %broadcast.133), dimensions={1}, to_apply=%all_to_all.56.reduce_sub_computation | reduce | bytes 3145732 | tf_op jit(solution)/shard_map/all_to_all | solution.py:40
  116.4 9.6 %reshape.82 = f32[1024,16,24]{2,1,0:T(8,128)} reshape(f32[4,98304]{1,0:T(4,128)S(1)} %reduce) | data formatting | bytes 3145728
  126.0 5.8 %copy.177 = f32[24,16,4,256]{3,2,1,0:T(4,128)S(1)} copy(f32[24,16,4,256]{0,1,3,2:T(8,128)} %bitcast.208) | data formatting | bytes 3145728 | tf_op jit(solution)/shard_map/all_to_all | solution.py:40
  133.7 5.1 %fusion.15 = (f32[96,1,16,256]{3,2,0,1:T(8,128)}, f32[96,16,256]{2,1,0:T(8,128)S(1)}, f32[96,16,256]{2,1,0:T(8,128)}) fusion(f32[96,16,256]{2,1,0:T(8,128)} %param.10, f32[96,16,256]{2,1,0:T(8,128)S(1)} %copy-done, f32[96,16,1]{2,1,0:T(8,128)} %copy.147, f32[96,16,255]{2,1,0:T(8,128)S(1)} %copy-done.23, f32[4,24,16,256]{3,2,1,0:T(8,128)S(1)} %copy.145, ...), kind=kLoop, calls=%fused_computation.39 | loop fusion | flops 4325376 | bytes 14155776 | tf_op jit(solution)/shard_map/stack | solution.py:22
  141.6 20.1 %collective-permute-start.3 = (f32[96,16,1]{0,1,2:T(8,128)S(1)}, f32[96,16,1]{0,1,2:T(8,128)S(1)}, u32[]{:S(2)}, u32[]{:S(2)}) collective-permute-start(f32[96,16,1]{0,1,2:T(8,128)S(1)} %copy.148), channel_id=1, source_target_pairs={{0,1},{1,2},{2,3},{4,5},{5,6},{6,7},{8,9},{9,10},{10,11},{12,13},{... | collective-permute-start | bytes 18440 | tf_op jit(solution)/shard_map/ppermute | solution.py:12
  166.0 3.6 subtract_bitcast_fusion.3
  173.0 3.2 convolution_select_fusion.15
  176.2 3.4 fusion.11
  179.6 3.6 fusion.10
  183.2 3.4 fusion.9
  198.1 4.1 %fusion.41 = (f32[96,16,256]{2,1,0:T(8,128)S(1)}, f32[96,16,256]{2,1,0:T(8,128)S(1)}) fusion(f32[96,16,256]{2,1,0:T(8,128)} %copy-done.6, f32[96,16,256]{2,1,0:T(8,128)S(1)} %multiply_add_fusion.3, f32[96,16,1]{2,1,0:T(8,128)} %copy.153, f32[96,16,255]{2,1,0:T(8,128)} %slice.213, f32[96,16,256]{2,1,0:T(8,128)} %get-tuple-element.32, ...), kind=kLoop, calls=%fused_computation.80 | loop fusion | flops 3145728 | bytes 11010048 | tf_op jit(solution)/shard_map/sub | solution.py:48
  203.5 3.6 collective-permute-start.5
  209.7 4.3 %collective-permute-start.7 = (f32[96,16,1]{0,1,2:T(8,128)S(1)}, f32[96,16,1]{0,1,2:T(8,128)S(1)}, u32[]{:S(2)}, u32[]{:S(2)}) collective-permute-start(f32[96,16,1]{0,1,2:T(8,128)S(1)} %copy.154), channel_id=1, source_target_pairs={{0,1},{1,2},{2,3},{4,5},{5,6},{6,7},{8,9},{9,10},{10,11},{12,13},{... | collective-permute-start | bytes 18440 | tf_op jit(solution)/shard_map/ppermute | solution.py:12
  216.4 4.3 %subtract_bitcast_fusion.2 = (f32[96,1,16,256]{3,2,0,1:T(8,128)S(1)}, f32[96,16,256]{2,1,0:T(8,128)S(1)}, f32[96,1,16,256]{3,2,0,1:T(8,128)S(1)}) fusion(f32[96,2,16,256]{3,2,1,0:T(8,128)} %bitcast.221, f32[96,16,256]{2,1,0:T(8,128)S(1)} %get-tuple-element.28, f32[96,16,255]{2,1,0:T(8,128)S(1)} %bitcast.211, f32[96,16,1]{2,1,0:T(8,128)} %copy.155, ...), kind=kLoop, calls=%fused_computation.105 | loop fusion | flops 4718592 | bytes 15745024 | tf_op jit(solution)/shard_map/stack | solution.py:22
  224.2 3.2 convolution_select_fusion.11
  227.4 3.4 fusion.8
  230.8 3.8 fusion.7
  234.6 3.4 fusion.6
  249.8 3.7 fusion.46
  259.4 4.3 %collective-permute-start.11 = (f32[96,16,1]{0,1,2:T(8,128)S(1)}, f32[96,16,1]{0,1,2:T(8,128)S(1)}, u32[]{:S(2)}, u32[]{:S(2)}) collective-permute-start(f32[96,16,1]{0,1,2:T(8,128)S(1)} %copy.161), channel_id=1, source_target_pairs={{0,1},{1,2},{2,3},{4,5},{5,6},{6,7},{8,9},{9,10},{10,11},{12,13},{... | collective-permute-start | bytes 18440 | tf_op jit(solution)/shard_map/ppermute | solution.py:12
  266.1 4.3 %subtract_bitcast_fusion.1 = (f32[96,1,16,256]{3,2,0,1:T(8,128)S(1)}, f32[96,16,256]{2,1,0:T(8,128)S(1)}, f32[96,1,16,256]{3,2,0,1:T(8,128)S(1)}) fusion(f32[96,2,16,256]{3,2,1,0:T(8,128)} %bitcast.218, f32[96,16,256]{2,1,0:T(8,128)S(1)} %copy-done.4, f32[96,16,255]{2,1,0:T(8,128)S(1)} %bitcast.212, f32[96,16,1]{2,1,0:T(8,128)} %copy.162, ...), kind=kLoop, calls=%fused_computation.103 | loop fusion | flops 4718592 | bytes 15745024 | tf_op jit(solution)/shard_map/stack | solution.py:22
  273.9 3.2 convolution_select_fusion.7
  277.0 3.4 fusion.5
  280.5 3.8 fusion.4
  284.3 3.4 fusion.3
  299.4 5.3 %fusion.50 = (f32[96,16,256]{2,1,0:T(8,128)}, f32[96,16,256]{2,1,0:T(8,128)}) fusion(f32[96,16,256]{2,1,0:T(8,128)S(1)} %copy-done.5, f32[96,16,256]{2,1,0:T(8,128)S(1)} %multiply_add_fusion.1, f32[96,16,1]{2,1,0:T(8,128)} %copy.168, f32[96,16,255]{2,1,0:T(8,128)} %slice.231, f32[96,16,256]{2,1,0:T(8,128)} %copy-done.14, ...), kind=kLoop, calls=%fused_computation.96 | loop fusion | flops 3145728 | bytes 11010048 | tf_op jit(solution)/shard_map/sub | solution.py:48
  304.7 5.4 %all-to-all-start.2 = ((f32[96,16,256]{2,1,0:T(8,128)}), f32[96,16,256]{2,1,0:T(8,128)}, u32[]{:S(2)}, u32[]{:S(2)}) async-start(f32[96,16,256]{2,1,0:T(8,128)} %get-tuple-element.25), calls=%async_computation.2 | async-start | bytes 3145728 | tf_op jit(solution)/shard_map/all_to_all | solution.py:58
  316.8 3.6 collective-permute-start.15
  320.5 16.2 %collective-permute-done.15 = f32[96,16,1]{0,1,2:T(8,128)S(1)} collective-permute-done((f32[96,16,1]{0,1,2:T(8,128)S(1)}, f32[96,16,1]{0,1,2:T(8,128)S(1)}, u32[]{:S(2)}, u32[]{:S(2)}) %collective-permute-start.15) | collective-permute-done | bytes 6176 | tf_op jit(solution)/shard_map/ppermute | solution.py:12
  337.9 6.3 %subtract_bitcast_fusion = (f32[96,1,16,256]{3,2,0,1:T(8,128)}, f32[96,16,256]{2,1,0:T(8,128)}, f32[96,1,16,256]{3,2,0,1:T(8,128)}) fusion(f32[96,2,16,256]{3,2,1,0:T(8,128)} %bitcast.215, f32[96,16,256]{2,1,0:T(8,128)} %get-tuple-element.24, f32[96,16,255]{2,1,0:T(8,128)} %bitcast.189, f32[96,16,1]{2,1,0:T(8,128)} %copy.171, ...), kind=kLoop, calls=%fused_computation.101 | loop fusion | flops 4718592 | bytes 15745024 | tf_op jit(solution)/shard_map/stack | solution.py:22
  344.2 4.3 %all-to-all-done.2 = f32[96,16,256]{2,1,0:T(8,128)} async-done(((f32[96,16,256]{2,1,0:T(8,128)}), f32[96,16,256]{2,1,0:T(8,128)}, u32[]{:S(2)}, u32[]{:S(2)}) %all-to-all-start.2) | async-done | bytes 1572896 | tf_op jit(solution)/shard_map/all_to_all | solution.py:58
  348.6 9.6 %all-to-all-start.3 = ((f32[96,16,256]{2,1,0:T(8,128)}), f32[96,16,256]{2,1,0:T(8,128)S(1)}, u32[]{:S(2)}, u32[]{:S(2)}) async-start(f32[96,16,256]{2,1,0:T(8,128)} %get-tuple-element.24), calls=%async_computation.3 | async-start | bytes 3145728 | tf_op jit(solution)/shard_map/all_to_all | solution.py:59
  363.4 3.2 convolution_select_fusion.3
  366.6 3.4 fusion.2
  370.0 3.6 fusion.1
  373.6 3.4 fusion
  385.1 10.1 %all-to-all-done.3 = f32[96,16,256]{2,1,0:T(8,128)S(1)} async-done(((f32[96,16,256]{2,1,0:T(8,128)}), f32[96,16,256]{2,1,0:T(8,128)S(1)}, u32[]{:S(2)}, u32[]{:S(2)}) %all-to-all-start.3) | async-done | bytes 1572896 | tf_op jit(solution)/shard_map/all_to_all | solution.py:59
  (153 shorter events, 101.9 us)
Async XLA Ops:
  17.3 6.5 %copy-start.26 = (f32[24,16,1024]{2,1,0:T(8,128)S(1)}, f32[24,16,1024]{2,1,0:T(8,128)}, u32[]{:S(2)}) copy-start(f32[24,16,1024]{2,1,0:T(8,128)} %param.8) | copy-start | bytes 4718596
  17.3 43.4 %all-to-all-start = ((f32[4,1,98304]{2,1,0:T(1,128)}), f32[4,1,98304]{2,1,0:T(1,128)S(1)}, u32[]{:S(2)}, u32[]{:S(2)}) async-start(f32[4,1,98304]{2,1,0:T(1,128)} %reshape.79), calls=%async_computation | async-start | bytes 3145728 | tf_op jit(solution)/shard_map/all_to_all | solution.py:39
  39.4 26.8 %copy-start = (f32[96,16,256]{2,1,0:T(8,128)S(1)}, f32[96,16,256]{2,1,0:T(8,128)}, u32[]{:S(2)}) copy-start(f32[96,16,256]{2,1,0:T(8,128)} %param.9) | copy-start | bytes 4718596
  61.8 48.4 %all-to-all-start.1 = ((f32[4,1,98304]{2,1,0:T(1,128)}), f32[4,1,98304]{2,1,0:T(1,128)}, u32[]{:S(2)}, u32[]{:S(2)}) async-start(f32[4,1,98304]{2,1,0:T(1,128)} %reshape.81), calls=%async_computation.1 | async-start | bytes 3145728 | tf_op jit(solution)/shard_map/all_to_all | solution.py:40
  66.2 1.5 slice-start
  66.3 65.8 %collective-permute-start = (f32[96,1,256]{2,1,0:T(1,128)S(1)}, f32[96,1,256]{2,1,0:T(1,128)S(1)}, u32[]{:S(2)}, u32[]{:S(2)}) collective-permute-start(f32[96,1,256]{2,1,0:T(1,128)S(1)} %slice.157), channel_id=1, source_target_pairs={{4,0},{8,4},{12,8},{16,12},{20,16},{24,20},{28,24},{5,1},{9,5},{13... | collective-permute-start | bytes 294920 | tf_op jit(solution)/shard_map/ppermute | solution.py:12
  68.1 17.1 %collective-permute-start.2 = (f32[96,16,1]{0,1,2:T(8,128)S(1)}, f32[96,16,1]{0,1,2:T(8,128)S(1)}, u32[]{:S(2)}, u32[]{:S(2)}) collective-permute-start(f32[96,16,1]{0,1,2:T(8,128)S(1)} %copy.178), channel_id=1, source_target_pairs={{1,0},{2,1},{3,2},{5,4},{6,5},{7,6},{9,8},{10,9},{11,10},{13,12},{... | collective-permute-start | bytes 18440 | tf_op jit(solution)/shard_map/ppermute | solution.py:12
  131.8 1.4 copy-start.22
  131.8 1.9 copy-start.23
  138.8 27.2 %copy-start.6 = (f32[96,16,256]{2,1,0:T(8,128)}, f32[96,16,256]{2,1,0:T(8,128)S(1)}, u32[]{:S(2)}) copy-start(f32[96,16,256]{2,1,0:T(8,128)S(1)} %get-tuple-element.31) | copy-start | bytes 4718596
  138.8 25.8 %copy-start.27 = (s32[16,256]{1,0:T(8,128)S(1)}, s32[16,256]{1,0:T(8,128)}, u32[]{:S(2)}) copy-start(s32[16,256]{1,0:T(8,128)} %param.12) | copy-start | bytes 49156
  141.6 23.1 %collective-permute-start.3 = (f32[96,16,1]{0,1,2:T(8,128)S(1)}, f32[96,16,1]{0,1,2:T(8,128)S(1)}, u32[]{:S(2)}, u32[]{:S(2)}) collective-permute-start(f32[96,16,1]{0,1,2:T(8,128)S(1)} %copy.148), channel_id=1, source_target_pairs={{0,1},{1,2},{2,3},{4,5},{5,6},{6,7},{8,9},{9,10},{10,11},{12,13},{... | collective-permute-start | bytes 18440 | tf_op jit(solution)/shard_map/ppermute | solution.py:12
  162.9 3.1 collective-permute-start.1
  166.0 3.6 copy-start.21
  170.3 2.7 copy-start.16
  186.6 1.4 copy-start.25
  187.9 1.6 copy-start.11
  189.6 8.5 %collective-permute-start.4 = (f32[96,1,256]{2,1,0:T(1,128)S(1)}, f32[96,1,256]{2,1,0:T(1,128)S(1)}, u32[]{:S(2)}, u32[]{:S(2)}) collective-permute-start(f32[96,1,256]{2,1,0:T(1,128)S(1)} %slice.210), channel_id=1, source_target_pairs={{4,0},{8,4},{12,8},{16,12},{20,16},{24,20},{28,24},{5,1},{9,5},{13... | collective-permute-start | bytes 294920 | tf_op jit(solution)/shard_map/ppermute | solution.py:12
  191.3 5.5 %collective-permute-start.6 = (f32[96,16,1]{0,1,2:T(8,128)S(1)}, f32[96,16,1]{0,1,2:T(8,128)S(1)}, u32[]{:S(2)}, u32[]{:S(2)}) collective-permute-start(f32[96,16,1]{0,1,2:T(8,128)S(1)} %copy.152), channel_id=1, source_target_pairs={{1,0},{2,1},{3,2},{5,4},{6,5},{7,6},{9,8},{10,9},{11,10},{13,12},{... | collective-permute-start | bytes 18440 | tf_op jit(solution)/shard_map/ppermute | solution.py:12
  202.2 1.1 copy-start.13
  202.2 14.2 %copy-start.1 = (f32[96,16,256]{2,1,0:T(8,128)}, f32[96,16,256]{2,1,0:T(8,128)S(1)}, u32[]{:S(2)}) copy-start(f32[96,16,256]{2,1,0:T(8,128)S(1)} %get-tuple-element.28) | copy-start | bytes 4718596
  203.5 13.0 %collective-permute-start.5 = (f32[96,1,256]{2,1,0:T(1,128)S(1)}, f32[96,1,256]{2,1,0:T(1,128)S(1)}, u32[]{:S(2)}, u32[]{:S(2)}) collective-permute-start(f32[96,1,256]{2,1,0:T(1,128)S(1)} %slice.211), channel_id=1, source_target_pairs={{0,4},{4,8},{8,12},{12,16},{16,20},{20,24},{24,28},{1,5},{5,9},{9,... | collective-permute-start | bytes 294920 | tf_op jit(solution)/shard_map/ppermute | solution.py:12
  209.7 5.5 %collective-permute-start.7 = (f32[96,16,1]{0,1,2:T(8,128)S(1)}, f32[96,16,1]{0,1,2:T(8,128)S(1)}, u32[]{:S(2)}, u32[]{:S(2)}) collective-permute-start(f32[96,16,1]{0,1,2:T(8,128)S(1)} %copy.154), channel_id=1, source_target_pairs={{0,1},{1,2},{2,3},{4,5},{5,6},{6,7},{8,9},{9,10},{10,11},{12,13},{... | collective-permute-start | bytes 18440 | tf_op jit(solution)/shard_map/ppermute | solution.py:12
  221.4 2.7 copy-start.17
  238.0 1.9 copy-start.12
  239.2 1.7 copy-start.9
  241.0 8.8 %collective-permute-start.8 = (f32[96,1,256]{2,1,0:T(1,128)S(1)}, f32[96,1,256]{2,1,0:T(1,128)S(1)}, u32[]{:S(2)}, u32[]{:S(2)}) collective-permute-start(f32[96,1,256]{2,1,0:T(1,128)S(1)} %slice.220), channel_id=1, source_target_pairs={{4,0},{8,4},{12,8},{16,12},{20,16},{24,20},{28,24},{5,1},{9,5},{13... | collective-permute-start | bytes 294920 | tf_op jit(solution)/shard_map/ppermute | solution.py:12
  242.7 5.8 %collective-permute-start.10 = (f32[96,16,1]{0,1,2:T(8,128)S(1)}, f32[96,16,1]{0,1,2:T(8,128)S(1)}, u32[]{:S(2)}, u32[]{:S(2)}) collective-permute-start(f32[96,16,1]{0,1,2:T(8,128)S(1)} %copy.159), channel_id=1, source_target_pairs={{1,0},{2,1},{3,2},{5,4},{6,5},{7,6},{9,8},{10,9},{11,10},{13,12},{... | collective-permute-start | bytes 18440 | tf_op jit(solution)/shard_map/ppermute | solution.py:12
  245.3 4.4 %copy-start.2 = (f32[96,16,256]{2,1,0:T(8,128)S(1)}, f32[96,16,256]{2,1,0:T(8,128)}, u32[]{:S(2)}) copy-start(f32[96,16,256]{2,1,0:T(8,128)} %copy-done.1) | copy-start | bytes 4718596
  253.4 3.2 copy-start.3
  253.4 3.2 copy-start.14
  253.6 12.5 %collective-permute-start.9 = (f32[96,1,256]{2,1,0:T(1,128)S(1)}, f32[96,1,256]{2,1,0:T(1,128)S(1)}, u32[]{:S(2)}, u32[]{:S(2)}) collective-permute-start(f32[96,1,256]{2,1,0:T(1,128)S(1)} %slice.221), channel_id=1, source_target_pairs={{0,4},{4,8},{8,12},{12,16},{16,20},{20,24},{24,28},{1,5},{5,9},{9,... | collective-permute-start | bytes 294920 | tf_op jit(solution)/shard_map/ppermute | solution.py:12
  257.8 8.3 %copy-start.4 = (f32[96,16,256]{2,1,0:T(8,128)S(1)}, f32[96,16,256]{2,1,0:T(8,128)}, u32[]{:S(2)}) copy-start(f32[96,16,256]{2,1,0:T(8,128)} %copy-done.3) | copy-start | bytes 4718596
  259.4 5.5 %collective-permute-start.11 = (f32[96,16,1]{0,1,2:T(8,128)S(1)}, f32[96,16,1]{0,1,2:T(8,128)S(1)}, u32[]{:S(2)}, u32[]{:S(2)}) collective-permute-start(f32[96,16,1]{0,1,2:T(8,128)S(1)} %copy.161), channel_id=1, source_target_pairs={{0,1},{1,2},{2,3},{4,5},{5,6},{6,7},{8,9},{9,10},{10,11},{12,13},{... | collective-permute-start | bytes 18440 | tf_op jit(solution)/shard_map/ppermute | solution.py:12
  271.1 2.7 copy-start.18
  287.7 1.9 copy-start.10
  288.9 1.6 copy-start.7
  290.6 8.8 %collective-permute-start.12 = (f32[96,1,256]{2,1,0:T(1,128)S(1)}, f32[96,1,256]{2,1,0:T(1,128)S(1)}, u32[]{:S(2)}, u32[]{:S(2)}) collective-permute-start(f32[96,1,256]{2,1,0:T(1,128)S(1)} %slice.230), channel_id=1, source_target_pairs={{4,0},{8,4},{12,8},{16,12},{20,16},{24,20},{28,24},{5,1},{9,5},{13... | collective-permute-start | bytes 294920 | tf_op jit(solution)/shard_map/ppermute | solution.py:12
  292.4 5.8 %collective-permute-start.13 = (f32[96,16,1]{0,1,2:T(8,128)S(1)}, f32[96,16,1]{0,1,2:T(8,128)S(1)}, u32[]{:S(2)}, u32[]{:S(2)}) collective-permute-start(f32[96,16,1]{0,1,2:T(8,128)S(1)} %copy.167), channel_id=1, source_target_pairs={{1,0},{2,1},{3,2},{5,4},{6,5},{7,6},{9,8},{10,9},{11,10},{13,12},{... | collective-permute-start | bytes 18440 | tf_op jit(solution)/shard_map/ppermute | solution.py:12
  295.0 4.4 %copy-start.5 = (f32[96,16,256]{2,1,0:T(8,128)S(1)}, f32[96,16,256]{2,1,0:T(8,128)}, u32[]{:S(2)}) copy-start(f32[96,16,256]{2,1,0:T(8,128)} %copy-done.3) | copy-start | bytes 4718596
  304.7 5.4 %copy-start.15 = (f32[96,16,256]{2,1,0:T(8,128)S(1)}, f32[96,16,256]{2,1,0:T(8,128)}, u32[]{:S(2)}) copy-start(f32[96,16,256]{2,1,0:T(8,128)} %get-tuple-element.25) | copy-start | bytes 4718596
  304.7 43.8 %all-to-all-start.2 = ((f32[96,16,256]{2,1,0:T(8,128)}), f32[96,16,256]{2,1,0:T(8,128)}, u32[]{:S(2)}, u32[]{:S(2)}) async-start(f32[96,16,256]{2,1,0:T(8,128)} %get-tuple-element.25), calls=%async_computation.2 | async-start | bytes 3145728 | tf_op jit(solution)/shard_map/all_to_all | solution.py:58
  310.2 27.7 %collective-permute-start.14 = (f32[96,1,256]{2,1,0:T(1,128)S(1)}, f32[96,1,256]{2,1,0:T(1,128)S(1)}, u32[]{:S(2)}, u32[]{:S(2)}) collective-permute-start(f32[96,1,256]{2,1,0:T(1,128)S(1)} %slice.233), channel_id=1, source_target_pairs={{0,4},{4,8},{8,12},{12,16},{16,20},{20,24},{24,28},{1,5},{5,9},{9,... | collective-permute-start | bytes 294920 | tf_op jit(solution)/shard_map/ppermute | solution.py:12
  316.8 19.9 %collective-permute-start.15 = (f32[96,16,1]{0,1,2:T(8,128)S(1)}, f32[96,16,1]{0,1,2:T(8,128)S(1)}, u32[]{:S(2)}, u32[]{:S(2)}) collective-permute-start(f32[96,16,1]{0,1,2:T(8,128)S(1)} %copy.170), channel_id=1, source_target_pairs={{0,1},{1,2},{2,3},{4,5},{5,6},{6,7},{8,9},{9,10},{10,11},{12,13},{... | collective-permute-start | bytes 18440 | tf_op jit(solution)/shard_map/ppermute | solution.py:12
  348.6 46.6 %all-to-all-start.3 = ((f32[96,16,256]{2,1,0:T(8,128)}), f32[96,16,256]{2,1,0:T(8,128)S(1)}, u32[]{:S(2)}, u32[]{:S(2)}) async-start(f32[96,16,256]{2,1,0:T(8,128)} %get-tuple-element.24), calls=%async_computation.3 | async-start | bytes 3145728 | tf_op jit(solution)/shard_map/all_to_all | solution.py:59
  360.7 2.7 copy-start.19
  377.1 1.9 copy-start.8
  377.1 2.3 copy-start.20
  (1 other events, 1.1 us)
where the time goes:
time: 403 us; the launch traced here: 397 us
  local copies, waits for them, and re-layouts  131 us (33%)
  starting transfers between devices  80.3 us (20%)
  waiting for transfers between devices  71 us (18%)
  other arithmetic  57.6 us (14%)
  matrix products  54.8 us (14%)
    unnamed x71, local copies, waits for them, and re-layouts  75.1 us
    dot_general x16, matrix products, column_update(): product = jnp.dot(inverses[klass], stacked, precision=lax.Precision.HIGHEST)  54.8 us
    ppermute x16, starting transfers between devices, from_behind(): lax.ppermute(value, axis, [(source, source + steps) for source in range(l...  54.5 us
    ppermute x16, waiting for transfers between devices, from_behind(): lax.ppermute(value, axis, [(source, source + steps) for source in range(l...  35.3 us
    another operation x9, other arithmetic, column_update(): jnp.stack([rhs_w, rhs_t], axis=1).reshape(2 * levels, columns_x * columns_y)  26.8 us
    all_to_all x1, waiting for transfers between devices, per_device(): lax.all_to_all(wind_u, 'gy', split_axis=2, concat_axis=0, tiled=True)  21.3 us
    sub x3, other arithmetic, per_device(): col_v = col_v - 0.5 * (next_y - pressure)  13.2 us
    slice x8, local copies, waits for them, and re-layouts, per_device(): edge_v = from_behind(col_v[:, :, -1:], 'gy', 1)  11.9 us
  transfers between devices with their start and end apart: 20, of which 10 were waited for; matrix products, arithmetic and copies ran while one was open for 32% of the time, Pallas kernels for 0%

commit v1 on v0

v1 whole, which is shorter than its diff:
```python
import functools

import jax
import jax.numpy as jnp
from jax import lax
from jax.experimental import pallas as pl
from jax.experimental.pallas import tpu as pltpu
from jax.sharding import PartitionSpec as P

SUBSTEPS = 4
MESH = pl.DeviceIdType.MESH
F32 = jnp.float32
BF16 = jnp.bfloat16


def kernel(dims, u_ref, v_ref, p_ref, w_ref, t_ref, terr_ref, inv_ref,
           uo_ref, vo_ref, po_ref, wo_ref, to_ref,
           u_buf, v_buf, p_buf, w_buf, t_buf, in_sem, out_sem,
           press, vert, theta, div, dsend, drecv, usend, uhalo,
           ysend, yhalo, ssend, srecv, shsend, shrecv, mats,
           d_s, d_r, u_s, u_r, y_s, y_r, x_s, x_r, s_s, s_r):
    ngx, ngy, nz, nx, ny, slab, classes = dims
    order = 2 * nz
    half = nx // 2
    turn = nx // 4
    wide = ngy * ny
    gx = lax.axis_index("gx")
    me = lax.axis_index("gy")
    has_left, has_right = gx > 0, gx < ngx - 1
    has_down, has_up = me > 0, me < ngy - 1

    def peer(r):
        return lax.rem(me + r, ngy)

    def at(dx, dy):
        return (gx + dx, me + dy)

    loads, stores = [], []
    for slot, (ref, buf, out) in enumerate((
            (u_ref, u_buf, uo_ref), (v_ref, v_buf, vo_ref), (p_ref, p_buf, po_ref),
            (w_ref, w_buf, wo_ref), (t_ref, t_buf, to_ref))):
        tiles = buf.shape[0]
        loads.append([pltpu.make_async_copy(
            ref.at[:, pl.ds(c * 128, 128)], buf.at[c], in_sem.at[slot, c]) for c in range(tiles)])
        stores.append([pltpu.make_async_copy(
            buf.at[c], out.at[:, pl.ds(c * 128, 128)], out_sem.at[slot, c]) for c in range(tiles)])

    def start(copies):
        for each in copies:
            each.start()

    def wait(copies):
        for each in copies:
            each.wait()

    def take(buf, i, count):
        parts = [buf[c, pl.ds(i, count, stride=nx), :] for c in range(buf.shape[0])]
        return jnp.concatenate(parts, axis=1)

    def put(buf, i, value):
        for c in range(buf.shape[0]):
            buf[c, pl.ds(i, value.shape[0], stride=nx), :] = value[:, c * 128:(c + 1) * 128]

    for each in loads:
        start(each)

    barrier = pltpu.get_barrier_semaphore()

    @pl.when(has_left)
    def _():
        pl.semaphore_signal(barrier, inc=1, device_id=at(-1, 0), device_id_type=MESH)

    @pl.when(has_right)
    def _():
        pl.semaphore_signal(barrier, inc=1, device_id=at(1, 0), device_id_type=MESH)

    for r in range(1, ngy):
        pl.semaphore_signal(barrier, inc=1, device_id=(gx, peer(r)), device_id_type=MESH)
    pl.semaphore_wait(barrier, ngy - 1 + has_left.astype(jnp.int32) + has_right.astype(jnp.int32))

    def copy(src, dst, send, recv, device):
        return pltpu.make_async_remote_copy(
            src_ref=src, dst_ref=dst, send_sem=send, recv_sem=recv,
            device_id=device, device_id_type=MESH)

    def x_copy(n, way):
        if way == 0:
            return copy(press.at[n, 1], press.at[n, nx + 1], x_s.at[n, 0], x_r.at[n, 0], at(-1, 0))
        return copy(press.at[n, nx], press.at[n, 0], x_s.at[n, 1], x_r.at[n, 1], at(1, 0))

    def y_copy(n, g, way):
        return copy(ysend.at[n, g, way], yhalo.at[n, g, way], y_s.at[n, g, way], y_r.at[n, g, way],
                    at(0, -1) if way == 0 else at(0, 1))

    def d_copy(g, r):
        return copy(dsend.at[g, peer(r)], drecv.at[g, me], d_s.at[g, r], d_r.at[g, r], (gx, peer(r)))

    def s_copy(g, r):
        return copy(ssend.at[g, peer(r)], srecv.at[g, me], s_s.at[g, r], s_r.at[g, r], (gx, peer(r)))

    def sh_copy(r):
        return copy(shsend.at[peer(r)], shrecv.at[me], s_s.at[2, r], s_r.at[2, r], (gx, peer(r)))

    def u_copy():
        return copy(usend, uhalo, u_s.at[0], u_r.at[0], at(1, 0))

    def x_start(n):
        pl.when(has_left)(lambda: x_copy(n, 0).start())
        pl.when(has_right)(lambda: x_copy(n, 1).start())

    def x_wait(n):
        @pl.when(has_right)
        def _():
            x_copy(n, 0).wait_recv()

        @pl.when(jnp.logical_not(has_right))
        def _():
            press[n, nx + 1] = jnp.zeros((nz, ny), F32)

        @pl.when(has_left)
        def _():
            x_copy(n, 1).wait_recv()

        @pl.when(jnp.logical_not(has_left))
        def _():
            press[n, 0] = press[n, 1]

    def y_start(n, g):
        pl.when(has_down)(lambda: y_copy(n, g, 0).start())
        pl.when(has_up)(lambda: y_copy(n, g, 1).start())

    def y_wait(n, g):
        pl.when(has_up)(lambda: y_copy(n, g, 0).wait_recv())
        pl.when(has_down)(lambda: y_copy(n, g, 1).wait_recv())

    lane = lax.broadcasted_iota(jnp.int32, (nz, 128), 1)
    lanes = lax.broadcasted_iota(jnp.int32, (nz, ny), 1)
    level = lax.broadcasted_iota(jnp.int32, (nz, ny), 0)
    wide_lane = lax.broadcasted_iota(jnp.int32, (slab, wide), 1)

    def plane(k):
        return lax.rem(k + turn, nx)

    def keep_edges(n, g, i, value):
        for way, column in ((0, 0), (1, ny - 1)):
            edge = jnp.broadcast_to(value[:, column:column + 1], (nz, 128))
            ysend[n, g, way] = jnp.where(lane == i, edge, ysend[n, g, way])

    def clear_edges(n, g):
        for way in (0, 1):
            ysend[n, g, way] = jnp.zeros((nz, 128), F32)

    wait(loads[0])
    usend[...] = take(u_buf, nx - 1, slab)
    pl.when(has_right)(lambda: u_copy().start())

    @pl.when(jnp.logical_not(has_left))
    def _():
        uhalo[...] = jnp.zeros((slab, wide), F32)

    for n in range(SUBSTEPS):
        for g in range(2):
            @pl.when(jnp.logical_not(has_up))
            def _():
                yhalo[n, g, 0] = jnp.zeros((nz, 128), F32)

            @pl.when(jnp.logical_not(has_down))
            def _():
                yhalo[n, g, 1] = jnp.zeros((nz, 128), F32)

    wait(loads[1])
    for g in range(2):
        if g == 1:
            pl.when(has_left)(lambda: u_copy().wait_recv())

        def first_div(kk, carry):
            i = plane(g * half + kk)
            here = take(u_buf, i, slab)
            left = take(u_buf, jnp.maximum(i - 1, 0), slab)
            if g == 1:
                left = jnp.where(i == 0, uhalo[...], left)
            v = take(v_buf, i, slab)
            left_v = jnp.where(wide_lane == 0, 0.0, pltpu.roll(v, 1, 1))
            d = here - left + (v - left_v)
            for q in range(ngy):
                dsend[g, q, kk] = d[:, q * ny:(q + 1) * ny]
            return carry

        lax.fori_loop(0, half, first_div, 0)
        for r in range(1, ngy):
            d_copy(g, r).start()
        drecv[g, me] = dsend[g, me]

    for each in loads[2:]:
        wait(each)
    for g in range(2):
        clear_edges(0, g)

        def relay(kk, carry):
            i = plane(g * half + kk)
            p = take(p_buf, i, nz)
            press[0, i + 1] = p
            vert[i] = take(w_buf, i, nz)
            theta[i] = take(t_buf, i, nz)
            keep_edges(0, g, i, p)
            return carry

        lax.fori_loop(0, half, relay, 0)
        y_start(0, g)
    x_start(0)

    rows = lax.broadcasted_iota(jnp.int32, (order, order), 0)
    cols = lax.broadcasted_iota(jnp.int32, (order, order), 1)

    def source(r):
        return jnp.where(r < nz, 2 * r, 2 * (r - nz) + 1)

    pick = (cols == source(rows)).astype(F32).astype(BF16)
    wide_rows = lax.broadcasted_iota(jnp.int32, (order, classes * order), 0)
    wide_cols = lax.broadcasted_iota(jnp.int32, (order, classes * order), 1)
    for part in range(2):
        total = jnp.zeros((order, classes * order), F32)
        for c in range(classes):
            a = inv_ref[c]
            a_hi = a.astype(BF16)
            a_part = a_hi if part == 0 else (a - a_hi.astype(F32)).astype(BF16)
            by_row = jnp.dot(pick, a_part, preferred_element_type=F32).astype(BF16)
            r = wide_cols - c * order
            place = (r >= 0) & (r < order) & (wide_rows == source(r))
            total = total + jnp.dot(by_row, place.astype(F32).astype(BF16), preferred_element_type=F32)
        mats[part * order:(part + 1) * order, :] = total.astype(BF16)

    for n in range(SUBSTEPS):
        last = n == SUBSTEPS - 1
        for g in range(2):
            if not last:
                clear_edges(n + 1, g)
            y_wait(n, g)
            if g == 1:
                x_wait(n)
            if n == 0:
                for r in range(1, ngy):
                    d_copy(g, r).wait_recv()
            if last and g == 1:
                edge = press[0, nx + 1]
                for m in range(1, SUBSTEPS):
                    edge = edge + press[m, nx + 1]
                for q in range(ngy):
                    shsend[q] = edge[q * slab:(q + 1) * slab]
                for r in range(1, ngy):
                    sh_copy(r).start()
                shrecv[me] = shsend[me]

            def substep(kk, carry):
                i = plane(g * half + kk)
                p = press[n, i + 1]
                up = pltpu.roll(p, ny - 1, 1)
                edge = pltpu.roll(yhalo[n, g, 0], 127 - i, 1)
                up = jnp.where(lanes == ny - 1, jnp.concatenate([edge] * (ny // 128), axis=1), up)
                down = pltpu.roll(p, 1, 1)
                edge = pltpu.roll(yhalo[n, g, 1], lax.rem(128 - i, 128), 1)
                edge = jnp.concatenate([edge] * (ny // 128), axis=1)
                edge = jnp.where(has_down, edge, p)
                down = jnp.where(lanes == 0, edge, down)
                if n == 0:
                    d = jnp.concatenate([drecv[g, q, kk] for q in range(ngy)], axis=0)
                else:
                    d = div[i]
                d = d - 0.5 * ((press[n, i + 2] - p) - (p - press[n, i]) + ((up - p) - (p - down)))
                if not last:
                    div[i] = d
                below = jnp.where(level == 0, 0.0, pltpu.roll(p, 1, 0))
                t = theta[i]
                rw = vert[i] - 0.5 * (p - below)
                rt = t - 0.5 * d
                s = jnp.concatenate([rw, rt], axis=0)
                hi = s.astype(BF16)
                lo = (s - hi.astype(F32)).astype(BF16)
                ground = terr_ref[pl.ds(i, 1), :]
                masks = [(ground == c).astype(F32).astype(BF16) for c in range(classes)]
                his = jnp.concatenate([hi * m for m in masks], axis=0)
                los = jnp.concatenate([lo * m for m in masks], axis=0)
                first = jnp.dot(mats[...], his, preferred_element_type=F32)
                second = jnp.dot(mats[:order, :], los, preferred_element_type=F32)
                solved = first[:order] + (first[order:] + second)
                st = solved[nz:]
                w = jnp.where(level >= ground, solved[:nz], 0.0)
                new_p = p - 0.3 * d + 0.5 * (st - t)
                if last:
                    put(p_buf, i, new_p)
                    put(w_buf, i, w)
                    put(t_buf, i, st)
                else:
                    press[n + 1, i + 1] = new_p
                    vert[i] = w
                    theta[i] = st
                    keep_edges(n + 1, g, i, new_p)
                if n == SUBSTEPS - 2:
                    total = new_p + p
                    for m in range(SUBSTEPS - 2):
                        total = total + press[m, i + 1]
                    for q in range(ngy):
                        ssend[g, q, kk] = total[q * slab:(q + 1) * slab]
                return carry

            lax.fori_loop(0, half, substep, 0)
            if not last:
                y_start(n + 1, g)
                if g == 1:
                    x_start(n + 1)
            if n == SUBSTEPS - 2:
                for r in range(1, ngy):
                    s_copy(g, r).start()
                srecv[g, me] = ssend[g, me]

    for each in stores[2:]:
        start(each)
    for g in range(2):
        for r in range(1, ngy):
            s_copy(g, r).wait_recv()
    for r in range(1, ngy):
        sh_copy(r).wait_recv()

    def summed(i):
        if i == nx:
            return jnp.concatenate([shrecv[q] for q in range(ngy)], axis=1)
        g, kk = divmod((i - turn) % nx, half)
        return jnp.concatenate([srecv[g, q, kk] for q in range(ngy)], axis=1)

    for i in range(nx):
        s = summed(i)
        ahead = jnp.where(wide_lane == wide - 1, 0.0, pltpu.roll(s, wide - 1, 1))
        put(u_buf, i, take(u_buf, i, slab) - 0.5 * (summed(i + 1) - s))
        put(v_buf, i, take(v_buf, i, slab) - 0.5 * (ahead - s))
    start(stores[0])
    start(stores[1])

    pl.when(has_right)(lambda: u_copy().wait_send())
    for n in range(SUBSTEPS):
        pl.when(has_left)(lambda: x_copy(n, 0).wait_send())
        pl.when(has_right)(lambda: x_copy(n, 1).wait_send())
        for g in range(2):
            pl.when(has_down)(lambda: y_copy(n, g, 0).wait_send())
            pl.when(has_up)(lambda: y_copy(n, g, 1).wait_send())
    for r in range(1, ngy):
        for g in range(2):
            d_copy(g, r).wait_send()
            s_copy(g, r).wait_send()
        sh_copy(r).wait_send()
    for each in stores:
        wait(each)


def per_device(wind_u, wind_v, pressure, vertical_w, theta, terrain, inverses):
    ngx, ngy = lax.axis_size("gx"), lax.axis_size("gy")
    nz, nx, ny = pressure.shape
    slab, _, wide = wind_u.shape
    classes = inverses.shape[0]
    order = 2 * nz
    half = nx // 2
    vmem = pl.BlockSpec(memory_space=pltpu.VMEM)
    hbm = pl.BlockSpec(memory_space=pl.ANY)
    slabs = jax.ShapeDtypeStruct((slab * nx, wide), F32)
    columns = jax.ShapeDtypeStruct((nz * nx, ny), F32)
    dma = pltpu.SemaphoreType.DMA
    outs = pl.pallas_call(
        functools.partial(kernel, (ngx, ngy, nz, nx, ny, slab, classes)),
        out_shape=(slabs, slabs, columns, columns, columns),
        in_specs=[hbm] * 5 + [vmem] * 2,
        out_specs=(hbm,) * 5,
        scratch_shapes=[
            pltpu.VMEM((wide // 128, slab * nx, 128), F32),
            pltpu.VMEM((wide // 128, slab * nx, 128), F32),
            pltpu.VMEM((ny // 128, nz * nx, 128), F32),
            pltpu.VMEM((ny // 128, nz * nx, 128), F32),
            pltpu.VMEM((ny // 128, nz * nx, 128), F32),
            dma((5, wide // 128)), dma((5, wide // 128)),
            pltpu.VMEM((SUBSTEPS, nx + 2, nz, ny), F32),
            pltpu.VMEM((nx, nz, ny), F32),
            pltpu.VMEM((nx, nz, ny), F32),
            pltpu.VMEM((nx, nz, ny), F32),
            pltpu.VMEM((2, ngy, half, slab, ny), F32),
            pltpu.VMEM((2, ngy, half, slab, ny), F32),
            pltpu.VMEM((slab, wide), F32),
            pltpu.VMEM((slab, wide), F32),
            pltpu.VMEM((SUBSTEPS, 2, 2, nz, 128), F32),
            pltpu.VMEM((SUBSTEPS, 2, 2, nz, 128), F32),
            pltpu.VMEM((2, ngy, half, slab, ny), F32),
            pltpu.VMEM((2, ngy, half, slab, ny), F32),
            pltpu.VMEM((ngy, slab, ny), F32),
            pltpu.VMEM((ngy, slab, ny), F32),
            pltpu.VMEM((2 * order, classes * order), BF16),
            dma((2, ngy)), dma((2, ngy)),
            dma((1,)), dma((1,)),
            dma((SUBSTEPS, 2, 2)), dma((SUBSTEPS, 2, 2)),
            dma((SUBSTEPS, 2)), dma((SUBSTEPS, 2)),
            dma((3, ngy)), dma((3, ngy)),
        ],
        compiler_params=pltpu.CompilerParams(
            collective_id=0, has_side_effects=True, vmem_limit_bytes=60 * 1024 * 1024),
        name="acoustic",
    )(
        wind_u.reshape(slab * nx, wide), wind_v.reshape(slab * nx, wide),
        pressure.reshape(nz * nx, ny), vertical_w.reshape(nz * nx, ny),
        theta.reshape(nz * nx, ny), terrain, inverses,
    )
    return (outs[0].reshape(slab, nx, wide), outs[1].reshape(slab, nx, wide),
            *(o.reshape(nz, nx, ny) for o in outs[2:]))


def solution(mesh):
    return jax.shard_map(
        per_device,
        mesh=mesh,
        in_specs=(
            P("gy", "gx", None),
            P("gy", "gx", None),
            P(None, "gx", "gy"),
            P(None, "gx", "gy"),
            P(None, "gx", "gy"),
            P("gx", "gy"),
            P(),
        ),
        out_specs=(
            P("gy", "gx", None),
            P("gy", "gx", None),
            P(None, "gx", "gy"),
            P(None, "gx", "gy"),
            P(None, "gx", "gy"),
        ),
        check_vma=False,
    )
```

time: 403 us -> 121 us (0.30); the launches traced: 397 us -> 121 us
  local copies, waits for them, and re-layouts: 131 us -> 9.92 us
  Pallas kernels: 0 us -> 110 us
  starting transfers between devices: 80.3 us -> 0 us
  waiting for transfers between devices: 71 us -> 0 us
  other arithmetic: 57.6 us -> 0 us
  matrix products: 54.8 us -> 0 us
    pallas_call x0 -> x1, Pallas kernels: none -> 110 us  [per_device(): pl.pallas_call(functools.partial(kernel, (ngx, ngy, nz, nx, ny, slab, cla...]
    unnamed x71 -> x13, local copies, waits for them, and re-layouts: 75.1 us -> 9.92 us
    dot_general x16 -> x0, matrix products: 54.8 us -> none  [column_update(): product = jnp.dot(inverses[klass], stacked, precision=lax.Precision.HIGHEST)]
    ppermute x16 -> x0, starting transfers between devices: 54.5 us -> none  [from_behind(): lax.ppermute(value, axis, [(source, source + steps) for source in range(l...]
    all_to_all x4 -> x0, waiting for transfers between devices: 35.7 us -> none  [the longest x1 21.3 us: per_device(): lax.all_to_all(wind_u, 'gy', split_axis=2, concat_axis=0, tiled=True)]
    ppermute x16 -> x0, waiting for transfers between devices: 35.3 us -> none  [from_behind(): lax.ppermute(value, axis, [(source, source + steps) for source in range(l...]
    slice x32 -> x0, local copies, waits for them, and re-layouts: 26.8 us -> none  [the longest x8 11.9 us: per_device(): edge_v = from_behind(col_v[:, :, -1:], 'gy', 1)]
    another operation x9 -> x0, other arithmetic: 26.8 us -> none  [column_update(): jnp.stack([rhs_w, rhs_t], axis=1).reshape(2 * levels, columns_x * columns_y)]
  transfers between devices with their start and end apart: 20 -> 0, of which waited for: 10 -> 0; matrix products, arithmetic and copies ran while one was open for 32% -> 0% of each run, Pallas kernels for 0% -> 0%
where the time goes in v1:
time: 121 us
  Pallas kernels  110 us (91%)
  local copies, waits for them, and re-layouts  9.92 us (8%)
    pallas_call x1, Pallas kernels, per_device(): pl.pallas_call(functools.partial(kernel, (ngx, ngy, nz, nx, ny, slab, cla...  110 us
    unnamed x13, local copies, waits for them, and re-layouts  9.92 us

profile of v1, /device:TPU:0, one launch (start us, length us, event | category | flops | bytes accessed | tf_op | source)
XLA Modules:
  0.0 121.0 jit_solution(16547066439139270636)
XLA Ops:
  0.6 110.4 %acoustic.1 = (f32[384,1024]{1,0:T(8,128)}, f32[384,1024]{1,0:T(8,128)}, f32[1536,256]{1,0:T(8,128)}, f32[1536,256]{1,0:T(8,128)}, f32[1536,256]{1,0:T(8,128)}) custom-call(f32[384,1024]{1,0:T(8,128)} %bitcast.15, f32[384,1024]{1,0:T(8,128)} %bitcast.16, f32[1536,256]{1,0:T(8,128)} %bitcast.17, f32[1536,256]{1,0:T(8,128)} %bitcast.18, f32[1536,256]{1,0:T(8,128)} %bitcast.19, ...), custom_call_target="tpu_custom_call" | custom-call | tf_op jit(solution)/shard_map/acoustic/pallas_call | solution.py:366
  111.0 0.0 copy-start.3
  111.0 2.8 %copy.17 = f32[24,16,1024]{2,1,0:T(8,128)} copy(f32[24,16,1024]{2,1,0:T(8,128)} %bitcast.14) | data formatting | bytes 3145728
  113.9 0.0 copy-done.3
  113.9 0.0 copy-start.2
  113.9 1.1 copy.18
  115.0 0.8 copy-done.2
  115.9 0.0 copy-start.1
  115.9 1.1 copy.19
  117.0 0.8 copy-done.1
  117.8 0.0 copy-start
  117.8 1.1 copy.20
  119.0 0.8 copy-done
  119.8 1.1 copy.21
Async XLA Ops:
  111.0 2.9 %copy-start.3 = (f32[384,1024]{1,0:T(8,128)S(1)}, f32[384,1024]{1,0:T(8,128)}, u32[]{:S(2)}) copy-start(f32[384,1024]{1,0:T(8,128)} %get-tuple-element.11) | copy-start | bytes 4718596
  113.9 2.0 %copy-start.2 = (f32[1536,256]{1,0:T(8,128)S(1)}, f32[1536,256]{1,0:T(8,128)}, u32[]{:S(2)}) copy-start(f32[1536,256]{1,0:T(8,128)} %get-tuple-element.12) | copy-start | bytes 4718596
  115.9 2.0 %copy-start.1 = (f32[1536,256]{1,0:T(8,128)S(1)}, f32[1536,256]{1,0:T(8,128)}, u32[]{:S(2)}) copy-start(f32[1536,256]{1,0:T(8,128)} %get-tuple-element.13) | copy-start | bytes 4718596
  117.8 2.0 %copy-start = (f32[1536,256]{1,0:T(8,128)S(1)}, f32[1536,256]{1,0:T(8,128)}, u32[]{:S(2)}) copy-start(f32[1536,256]{1,0:T(8,128)} %get-tuple-element.14) | copy-start | bytes 4718596

commit v2 on v1

--- a/solution.py
+++ b/solution.py
@@ -14,15 +14,15 @@
 
 
 def kernel(dims, u_ref, v_ref, p_ref, w_ref, t_ref, terr_ref, inv_ref,
-           uo_ref, vo_ref, po_ref, wo_ref, to_ref,
-           u_buf, v_buf, p_buf, w_buf, t_buf, in_sem, out_sem,
+           u_buf, v_buf, p_buf, w_buf, t_buf, in_sem,
            press, vert, theta, div, dsend, drecv, usend, uhalo,
            ysend, yhalo, ssend, srecv, shsend, shrecv, mats,
            d_s, d_r, u_s, u_r, y_s, y_r, x_s, x_r, s_s, s_r):
     ngx, ngy, nz, nx, ny, slab, classes = dims
     order = 2 * nz
     half = nx // 2
-    turn = nx // 4
+    quarter = nx // 4
+    turn = quarter
     wide = ngy * ny
     gx = lax.axis_index("gx")
     me = lax.axis_index("gy")
@@ -35,15 +35,12 @@
     def at(dx, dy):
         return (gx + dx, me + dy)
 
-    loads, stores = [], []
-    for slot, (ref, buf, out) in enumerate((
-            (u_ref, u_buf, uo_ref), (v_ref, v_buf, vo_ref), (p_ref, p_buf, po_ref),
-            (w_ref, w_buf, wo_ref), (t_ref, t_buf, to_ref))):
+    loads = []
+    for slot, (ref, buf) in enumerate((
+            (u_ref, u_buf), (v_ref, v_buf), (p_ref, p_buf), (w_ref, w_buf), (t_ref, t_buf))):
         tiles = buf.shape[0]
         loads.append([pltpu.make_async_copy(
             ref.at[:, pl.ds(c * 128, 128)], buf.at[c], in_sem.at[slot, c]) for c in range(tiles)])
-        stores.append([pltpu.make_async_copy(
-            buf.at[c], out.at[:, pl.ds(c * 128, 128)], out_sem.at[slot, c]) for c in range(tiles)])
 
     def start(copies):
         for each in copies:
@@ -99,7 +96,7 @@
         return copy(ssend.at[g, peer(r)], srecv.at[g, me], s_s.at[g, r], s_r.at[g, r], (gx, peer(r)))
 
     def sh_copy(r):
-        return copy(shsend.at[peer(r)], shrecv.at[me], s_s.at[2, r], s_r.at[2, r], (gx, peer(r)))
+        return copy(shsend.at[peer(r)], shrecv.at[me], s_s.at[4, r], s_r.at[4, r], (gx, peer(r)))
 
     def u_copy():
         return copy(usend, uhalo, u_s.at[0], u_r.at[0], at(1, 0))
@@ -169,15 +166,15 @@
                 yhalo[n, g, 1] = jnp.zeros((nz, 128), F32)
 
     wait(loads[1])
-    for g in range(2):
-        if g == 1:
+    for g in range(4):
+        if g == 3:
             pl.when(has_left)(lambda: u_copy().wait_recv())
 
         def first_div(kk, carry):
-            i = plane(g * half + kk)
+            i = plane(g * quarter + kk)
             here = take(u_buf, i, slab)
             left = take(u_buf, jnp.maximum(i - 1, 0), slab)
-            if g == 1:
+            if g == 3:
                 left = jnp.where(i == 0, uhalo[...], left)
             v = take(v_buf, i, slab)
             left_v = jnp.where(wide_lane == 0, 0.0, pltpu.roll(v, 1, 1))
@@ -186,7 +183,7 @@
                 dsend[g, q, kk] = d[:, q * ny:(q + 1) * ny]
             return carry
 
-        lax.fori_loop(0, half, first_div, 0)
+        lax.fori_loop(0, quarter, first_div, 0, unroll=2)
         for r in range(1, ngy):
             d_copy(g, r).start()
         drecv[g, me] = dsend[g, me]
@@ -205,7 +202,7 @@
             keep_edges(0, g, i, p)
             return carry
 
-        lax.fori_loop(0, half, relay, 0)
+        lax.fori_loop(0, half, relay, 0, unroll=2)
         y_start(0, g)
     x_start(0)
 
@@ -235,13 +232,9 @@
         for g in range(2):
             if not last:
                 clear_edges(n + 1, g)
-            y_wait(n, g)
-            if g == 1:
+            if g == (0 if last else 1):
                 x_wait(n)
-            if n == 0:
-                for r in range(1, ngy):
-                    d_copy(g, r).wait_recv()
-            if last and g == 1:
+            if last and g == 0:
                 edge = press[0, nx + 1]
                 for m in range(1, SUBSTEPS):
                     edge = edge + press[m, nx + 1]
@@ -250,9 +243,10 @@
                 for r in range(1, ngy):
                     sh_copy(r).start()
                 shrecv[me] = shsend[me]
-
-            def substep(kk, carry):
-                i = plane(g * half + kk)
+            y_wait(n, g)
+
+            def substep(h, kk, carry):
+                i = plane(h * quarter + kk)
                 p = press[n, i + 1]
                 up = pltpu.roll(p, ny - 1, 1)
                 edge = pltpu.roll(yhalo[n, g, 0], 127 - i, 1)
@@ -263,7 +257,7 @@
                 edge = jnp.where(has_down, edge, p)
                 down = jnp.where(lanes == 0, edge, down)
                 if n == 0:
-                    d = jnp.concatenate([drecv[g, q, kk] for q in range(ngy)], axis=0)
+                    d = jnp.concatenate([drecv[h, q, kk] for q in range(ngy)], axis=0)
                 else:
                     d = div[i]
                 d = d - 0.5 * ((press[n, i + 2] - p) - (p - press[n, i]) + ((up - p) - (p - down)))
@@ -300,40 +294,45 @@
                     for m in range(SUBSTEPS - 2):
                         total = total + press[m, i + 1]
                     for q in range(ngy):
-                        ssend[g, q, kk] = total[q * slab:(q + 1) * slab]
+                        ssend[h, q, kk] = total[q * slab:(q + 1) * slab]
                 return carry
 
-            lax.fori_loop(0, half, substep, 0)
-            if not last:
-                y_start(n + 1, g)
-                if g == 1:
-                    x_start(n + 1)
-            if n == SUBSTEPS - 2:
-                for r in range(1, ngy):
-                    s_copy(g, r).start()
-                srecv[g, me] = ssend[g, me]
-
-    for each in stores[2:]:
-        start(each)
-    for g in range(2):
-        for r in range(1, ngy):
-            s_copy(g, r).wait_recv()
-    for r in range(1, ngy):
-        sh_copy(r).wait_recv()
+            for h in (2 * g, 2 * g + 1):
+                if n == 0:
+                    for r in range(1, ngy):
+                        d_copy(h, r).wait_recv()
+                lax.fori_loop(0, quarter, functools.partial(substep, h), 0, unroll=2)
+                if not last and h == 2 * g + 1:
+                    y_start(n + 1, g)
+                    if g == 1:
+                        x_start(n + 1)
+                if n == SUBSTEPS - 2:
+                    for r in range(1, ngy):
+                        s_copy(h, r).start()
+                    srecv[h, me] = ssend[h, me]
 
     def summed(i):
         if i == nx:
             return jnp.concatenate([shrecv[q] for q in range(ngy)], axis=1)
-        g, kk = divmod((i - turn) % nx, half)
+        g, kk = divmod((i - turn) % nx, quarter)
         return jnp.concatenate([srecv[g, q, kk] for q in range(ngy)], axis=1)
 
-    for i in range(nx):
+    def finish(i):
         s = summed(i)
         ahead = jnp.where(wide_lane == wide - 1, 0.0, pltpu.roll(s, wide - 1, 1))
         put(u_buf, i, take(u_buf, i, slab) - 0.5 * (summed(i + 1) - s))
         put(v_buf, i, take(v_buf, i, slab) - 0.5 * (ahead - s))
-    start(stores[0])
-    start(stores[1])
+
+    for g in range(4):
+        for r in range(1, ngy):
+            s_copy(g, r).wait_recv()
+        for k in range(max(g * quarter - 1, 0), (g + 1) * quarter - 1):
+            if k != nx - 1 - turn:
+                finish((k + turn) % nx)
+    finish(turn - 1)
+    for r in range(1, ngy):
+        sh_copy(r).wait_recv()
+    finish(nx - 1)
 
     pl.when(has_right)(lambda: u_copy().wait_send())
     for n in range(SUBSTEPS):
@@ -343,12 +342,21 @@
             pl.when(has_down)(lambda: y_copy(n, g, 0).wait_send())
             pl.when(has_up)(lambda: y_copy(n, g, 1).wait_send())
     for r in range(1, ngy):
-        for g in range(2):
+        for g in range(4):
             d_copy(g, r).wait_send()
             s_copy(g, r).wait_send()
         sh_copy(r).wait_send()
-    for each in stores:
-        wait(each)
+
+
+def write_out(*refs):
+    ins, outs, sem = refs[:5], refs[5:10], refs[10]
+    copies = [
+        pltpu.make_async_copy(buf.at[c], out.at[:, pl.ds(c * 128, 128)], sem.at[slot, c])
+        for slot, (buf, out) in enumerate(zip(ins, outs)) for c in range(buf.shape[0])]
+    for each in copies:
+        each.start()
+    for each in copies:
+        each.wait()
 
 
 def per_device(wind_u, wind_v, pressure, vertical_w, theta, terrain, inverses):
@@ -357,53 +365,57 @@
     slab, _, wide = wind_u.shape
     classes = inverses.shape[0]
     order = 2 * nz
-    half = nx // 2
+    quarter = nx // 4
     vmem = pl.BlockSpec(memory_space=pltpu.VMEM)
-    hbm = pl.BlockSpec(memory_space=pl.ANY)
-    slabs = jax.ShapeDtypeStruct((slab * nx, wide), F32)
-    columns = jax.ShapeDtypeStruct((nz * nx, ny), F32)
+    hbm = pl.BlockSpec(memory_space=pltpu.HBM)
+    slabs = jax.ShapeDtypeStruct((wide // 128, slab * nx, 128), F32)
+    columns = jax.ShapeDtypeStruct((ny // 128, nz * nx, 128), F32)
     dma = pltpu.SemaphoreType.DMA
     outs = pl.pallas_call(
         functools.partial(kernel, (ngx, ngy, nz, nx, ny, slab, classes)),
         out_shape=(slabs, slabs, columns, columns, columns),
         in_specs=[hbm] * 5 + [vmem] * 2,
-        out_specs=(hbm,) * 5,
+        out_specs=(vmem,) * 5,
         scratch_shapes=[
-            pltpu.VMEM((wide // 128, slab * nx, 128), F32),
-            pltpu.VMEM((wide // 128, slab * nx, 128), F32),
-            pltpu.VMEM((ny // 128, nz * nx, 128), F32),
-            pltpu.VMEM((ny // 128, nz * nx, 128), F32),
-            pltpu.VMEM((ny // 128, nz * nx, 128), F32),
-            dma((5, wide // 128)), dma((5, wide // 128)),
+            dma((5, wide // 128)),
             pltpu.VMEM((SUBSTEPS, nx + 2, nz, ny), F32),
             pltpu.VMEM((nx, nz, ny), F32),
             pltpu.VMEM((nx, nz, ny), F32),
             pltpu.VMEM((nx, nz, ny), F32),
-            pltpu.VMEM((2, ngy, half, slab, ny), F32),
-            pltpu.VMEM((2, ngy, half, slab, ny), F32),
+            pltpu.VMEM((4, ngy, quarter, slab, ny), F32),
+            pltpu.VMEM((4, ngy, quarter, slab, ny), F32),
             pltpu.VMEM((slab, wide), F32),
             pltpu.VMEM((slab, wide), F32),
             pltpu.VMEM((SUBSTEPS, 2, 2, nz, 128), F32),
             pltpu.VMEM((SUBSTEPS, 2, 2, nz, 128), F32),
-            pltpu.VMEM((2, ngy, half, slab, ny), F32),
-            pltpu.VMEM((2, ngy, half, slab, ny), F32),
+            pltpu.VMEM((4, ngy, quarter, slab, ny), F32),
+            pltpu.VMEM((4, ngy, quarter, slab, ny), F32),
             pltpu.VMEM((ngy, slab, ny), F32),
             pltpu.VMEM((ngy, slab, ny), F32),
             pltpu.VMEM((2 * order, classes * order), BF16),
-            dma((2, ngy)), dma((2, ngy)),
+            dma((4, ngy)), dma((4, ngy)),
             dma((1,)), dma((1,)),
             dma((SUBSTEPS, 2, 2)), dma((SUBSTEPS, 2, 2)),
             dma((SUBSTEPS, 2)), dma((SUBSTEPS, 2)),
-            dma((3, ngy)), dma((3, ngy)),
+            dma((5, ngy)), dma((5, ngy)),
         ],
         compiler_params=pltpu.CompilerParams(
-            collective_id=0, has_side_effects=True, vmem_limit_bytes=60 * 1024 * 1024),
+            collective_id=0, has_side_effects=True, vmem_limit_bytes=52 * 1024 * 1024),
         name="acoustic",
     )(
         wind_u.reshape(slab * nx, wide), wind_v.reshape(slab * nx, wide),
         pressure.reshape(nz * nx, ny), vertical_w.reshape(nz * nx, ny),
         theta.reshape(nz * nx, ny), terrain, inverses,
     )
+    outs = pl.pallas_call(
+        write_out,
+        out_shape=tuple(jax.ShapeDtypeStruct((o.shape[1], o.shape[0] * 128), F32) for o in outs),
+        in_specs=[vmem] * 5,
+        out_specs=(hbm,) * 5,
+        scratch_shapes=[dma((5, wide // 128))],
+        compiler_params=pltpu.CompilerParams(vmem_limit_bytes=16 * 1024 * 1024),
+        name="write_out",
+    )(*outs)
     return (outs[0].reshape(slab, nx, wide), outs[1].reshape(slab, nx, wide),
             *(o.reshape(nz, nx, ny) for o in outs[2:]))
 

time: 121 us -> 125 us (1.033)
  Pallas kernels: 110 us -> 114 us
    pallas_call x0 -> x1, Pallas kernels: none -> 3.49 us  [per_device(): pl.pallas_call(write_out, out_shape=tuple((jax.ShapeDtypeStruct((o.shape[...]
    unnamed x13 -> x14, local copies, waits for them, and re-layouts: 9.92 us -> 8.87 us
where the time goes in v2:
time: 125 us; the launch traced here: 124 us
  Pallas kernels  114 us (91%)
  local copies, waits for them, and re-layouts  8.87 us (7%)
    pallas_call x1, Pallas kernels, per_device(): pl.pallas_call(functools.partial(kernel, (ngx, ngy, nz, nx, ny, slab, cla...  111 us
    unnamed x14, local copies, waits for them, and re-layouts  8.87 us
    pallas_call x1, Pallas kernels, per_device(): pl.pallas_call(write_out, out_shape=tuple((jax.ShapeDtypeStruct((o.shape[...  3.49 us

profile of v2, /device:TPU:0, one launch (start us, length us, event | category | flops | bytes accessed | tf_op | source)
XLA Modules:
  0.0 124.0 jit_solution(15189602725574787046)
XLA Ops:
  0.6 0.0 copy-start.5
  0.6 1.1 copy-done.5
  1.8 0.0 copy-start.6
  1.8 0.7 copy-done.6
  2.5 110.8 %acoustic.1 = (f32[8,384,128]{2,1,0:T(8,128)}, f32[8,384,128]{2,1,0:T(8,128)}, f32[2,1536,128]{2,1,0:T(8,128)}, f32[2,1536,128]{2,1,0:T(8,128)}, f32[2,1536,128]{2,1,0:T(8,128)}) custom-call(f32[384,1024]{1,0:T(8,128)} %bitcast.10, f32[384,1024]{1,0:T(8,128)} %bitcast.11, f32[1536,256]{1,0:T(8,128)} %bitcast.12, f32[1536,256]{1,0:T(8,128)} %bitcast.13, ...), custom_call_target="tpu_custom_call" | custom-call | tf_op jit(solution)/shard_map/acoustic/pallas_call | solution.py:374
  113.3 0.0 copy-start
  113.3 1.4 %copy-done = f32[8,384,128]{2,1,0:T(8,128)S(1)} copy-done((f32[8,384,128]{2,1,0:T(8,128)S(1)}, f32[8,384,128]{2,1,0:T(8,128)}, u32[]{:S(2)}) %copy-start) | copy-done | bytes 1572888
  114.7 0.0 copy-start.1
  114.7 1.4 %copy-done.1 = f32[8,384,128]{2,1,0:T(8,128)S(1)} copy-done((f32[8,384,128]{2,1,0:T(8,128)S(1)}, f32[8,384,128]{2,1,0:T(8,128)}, u32[]{:S(2)}) %copy-start.1) | copy-done | bytes 1572888
  116.1 0.0 copy-start.2
  116.1 1.4 %copy-done.2 = f32[2,1536,128]{2,1,0:T(8,128)S(1)} copy-done((f32[2,1536,128]{2,1,0:T(8,128)S(1)}, f32[2,1536,128]{2,1,0:T(8,128)}, u32[]{:S(2)}) %copy-start.2) | copy-done | bytes 1572888
  117.6 0.0 copy-start.3
  117.6 1.4 %copy-done.3 = f32[2,1536,128]{2,1,0:T(8,128)S(1)} copy-done((f32[2,1536,128]{2,1,0:T(8,128)S(1)}, f32[2,1536,128]{2,1,0:T(8,128)}, u32[]{:S(2)}) %copy-start.3) | copy-done | bytes 1572888
  119.0 0.0 copy-start.4
  119.0 1.4 %copy-done.4 = f32[2,1536,128]{2,1,0:T(8,128)S(1)} copy-done((f32[2,1536,128]{2,1,0:T(8,128)S(1)}, f32[2,1536,128]{2,1,0:T(8,128)}, u32[]{:S(2)}) %copy-start.4) | copy-done | bytes 1572888
  120.4 3.5 %write_out.1 = (f32[384,1024]{1,0:T(8,128)}, f32[384,1024]{1,0:T(8,128)}, f32[1536,256]{1,0:T(8,128)}, f32[1536,256]{1,0:T(8,128)}, f32[1536,256]{1,0:T(8,128)}) custom-call(f32[8,384,128]{2,1,0:T(8,128)S(1)} %copy-done, f32[8,384,128]{2,1,0:T(8,128)S(1)} %copy-done.1, f32[2,1536,128]{2,1,0:T(8,128)S(1)} %copy-done.2, f32[2,1536,128]{2,1,0:T(8,128)S(1)} %copy-done.3, ...), custom_call_target="tpu_custom_call" | custom-call | tf_op jit(solution)/shard_map/write_out/pallas_call | solution.py:410
Async XLA Ops:
  0.6 1.1 copy-start.5
  1.8 0.7 copy-start.6
  113.3 1.4 %copy-start = (f32[8,384,128]{2,1,0:T(8,128)S(1)}, f32[8,384,128]{2,1,0:T(8,128)}, u32[]{:S(2)}) copy-start(f32[8,384,128]{2,1,0:T(8,128)} %get-tuple-element.15.refs_0_) | copy-start | bytes 4718596
  114.7 1.4 %copy-start.1 = (f32[8,384,128]{2,1,0:T(8,128)S(1)}, f32[8,384,128]{2,1,0:T(8,128)}, u32[]{:S(2)}) copy-start(f32[8,384,128]{2,1,0:T(8,128)} %get-tuple-element.16.refs_1_) | copy-start | bytes 4718596
  116.1 1.4 %copy-start.2 = (f32[2,1536,128]{2,1,0:T(8,128)S(1)}, f32[2,1536,128]{2,1,0:T(8,128)}, u32[]{:S(2)}) copy-start(f32[2,1536,128]{2,1,0:T(8,128)} %get-tuple-element.17.refs_2_) | copy-start | bytes 4718596
  117.6 1.4 %copy-start.3 = (f32[2,1536,128]{2,1,0:T(8,128)S(1)}, f32[2,1536,128]{2,1,0:T(8,128)}, u32[]{:S(2)}) copy-start(f32[2,1536,128]{2,1,0:T(8,128)} %get-tuple-element.18.refs_3_) | copy-start | bytes 4718596
  119.0 1.4 %copy-start.4 = (f32[2,1536,128]{2,1,0:T(8,128)S(1)}, f32[2,1536,128]{2,1,0:T(8,128)}, u32[]{:S(2)}) copy-start(f32[2,1536,128]{2,1,0:T(8,128)} %get-tuple-element.19.refs_4_) | copy-start | bytes 4718596

commit v3 on v2

--- a/solution.py
+++ b/solution.py
@@ -13,8 +13,8 @@
 BF16 = jnp.bfloat16
 
 
-def kernel(dims, u_ref, v_ref, p_ref, w_ref, t_ref, terr_ref, inv_ref,
-           u_buf, v_buf, p_buf, w_buf, t_buf, in_sem,
+def kernel(dims, u_ref, v_ref, p_ref, w_ref, t_ref, terr_hbm, inv_hbm,
+           u_buf, v_buf, p_buf, w_buf, t_buf, terr_ref, inv_ref, in_sem, small_sem,
            press, vert, theta, div, dsend, drecv, usend, uhalo,
            ysend, yhalo, ssend, srecv, shsend, shrecv, mats,
            d_s, d_r, u_s, u_r, y_s, y_r, x_s, x_r, s_s, s_r):
@@ -58,6 +58,10 @@
         for c in range(buf.shape[0]):
             buf[c, pl.ds(i, value.shape[0], stride=nx), :] = value[:, c * 128:(c + 1) * 128]
 
+    loads.append([
+        pltpu.make_async_copy(terr_hbm, terr_ref, small_sem.at[0]),
+        pltpu.make_async_copy(inv_hbm, inv_ref, small_sem.at[1]),
+    ])
     for each in loads:
         start(each)
 
@@ -187,24 +191,25 @@
         for r in range(1, ngy):
             d_copy(g, r).start()
         drecv[g, me] = dsend[g, me]
-
-    for each in loads[2:]:
-        wait(each)
-    for g in range(2):
-        clear_edges(0, g)
-
-        def relay(kk, carry):
-            i = plane(g * half + kk)
-            p = take(p_buf, i, nz)
-            press[0, i + 1] = p
-            vert[i] = take(w_buf, i, nz)
-            theta[i] = take(t_buf, i, nz)
-            keep_edges(0, g, i, p)
-            return carry
-
-        lax.fori_loop(0, half, relay, 0, unroll=2)
-        y_start(0, g)
-    x_start(0)
+        if g == 0:
+            for each in loads[2:]:
+                wait(each)
+            for part in range(2):
+                clear_edges(0, part)
+
+                def relay(kk, carry):
+                    i = plane(part * half + kk)
+                    p = take(p_buf, i, nz)
+                    press[0, i + 1] = p
+                    vert[i] = take(w_buf, i, nz)
+                    theta[i] = take(t_buf, i, nz)
+                    keep_edges(0, part, i, p)
+                    return carry
+
+                lax.fori_loop(0, half, relay, 0, unroll=2)
+                y_start(0, part)
+            x_start(0)
+
 
     rows = lax.broadcasted_iota(jnp.int32, (order, order), 0)
     cols = lax.broadcasted_iota(jnp.int32, (order, order), 1)
@@ -301,7 +306,7 @@
                 if n == 0:
                     for r in range(1, ngy):
                         d_copy(h, r).wait_recv()
-                lax.fori_loop(0, quarter, functools.partial(substep, h), 0, unroll=2)
+                lax.fori_loop(0, quarter, functools.partial(substep, h), 0, unroll=4)
                 if not last and h == 2 * g + 1:
                     y_start(n + 1, g)
                     if g == 1:
@@ -374,10 +379,12 @@
     outs = pl.pallas_call(
         functools.partial(kernel, (ngx, ngy, nz, nx, ny, slab, classes)),
         out_shape=(slabs, slabs, columns, columns, columns),
-        in_specs=[hbm] * 5 + [vmem] * 2,
+        in_specs=[hbm] * 7,
         out_specs=(vmem,) * 5,
         scratch_shapes=[
-            dma((5, wide // 128)),
+            pltpu.VMEM((nx, ny), jnp.int32),
+            pltpu.VMEM((classes, order, order), F32),
+            dma((5, wide // 128)), dma((2,)),
             pltpu.VMEM((SUBSTEPS, nx + 2, nz, ny), F32),
             pltpu.VMEM((nx, nz, ny), F32),
             pltpu.VMEM((nx, nz, ny), F32),
@@ -400,7 +407,7 @@
             dma((5, ngy)), dma((5, ngy)),
         ],
         compiler_params=pltpu.CompilerParams(
-            collective_id=0, has_side_effects=True, vmem_limit_bytes=52 * 1024 * 1024),
+            collective_id=0, has_side_effects=True, vmem_limit_bytes=45 * 1024 * 1024),
         name="acoustic",
     )(
         wind_u.reshape(slab * nx, wide), wind_v.reshape(slab * nx, wide),

time: 125 us -> 99.4 us (0.80)
  Pallas kernels: 114 us -> 96.5 us
  local copies, waits for them, and re-layouts: 8.87 us -> 1.84 us
    pallas_call x1, Pallas kernels: 111 us -> 93 us  [per_device(): pl.pallas_call(functools.partial(kernel, (ngx, ngy, nz, nx, ny, slab, cla...]
    unnamed x14 -> x4, local copies, waits for them, and re-layouts: 8.87 us -> 1.84 us
where the time goes in v3:
time: 99.4 us; the launch traced here: 99.2 us
  Pallas kernels  96.5 us (97%)
  local copies, waits for them, and re-layouts  1.84 us (2%)
    pallas_call x1, Pallas kernels, per_device(): pl.pallas_call(functools.partial(kernel, (ngx, ngy, nz, nx, ny, slab, cla...  93 us
    pallas_call x1, Pallas kernels, per_device(): pl.pallas_call(write_out, out_shape=tuple((jax.ShapeDtypeStruct((o.shape[...  3.5 us

profile of v3, /device:TPU:0, one launch (start us, length us, event | category | flops | bytes accessed | tf_op | source)
XLA Modules:
  0.0 99.2 jit_solution(2053407535677760680)
XLA Ops:
  0.6 0.0 copy-start
  0.6 1.1 %copy-done = f32[4,192,192]{2,1,0:T(8,128)S(1)} copy-done((f32[4,192,192]{2,1,0:T(8,128)S(1)}, f32[4,192,192]{2,1,0:T(8,128)}, u32[]{:S(2)}) %copy-start) | copy-done | bytes 589848
  1.8 0.0 copy-start.1
  1.8 0.7 copy-done.1
  2.5 93.0 %acoustic.1 = (f32[8,384,128]{2,1,0:T(8,128)S(1)}, f32[8,384,128]{2,1,0:T(8,128)S(1)}, f32[2,1536,128]{2,1,0:T(8,128)S(1)}, f32[2,1536,128]{2,1,0:T(8,128)S(1)}, f32[2,1536,128]{2,1,0:T(8,128)S(1)}) custom-call(f32[384,1024]{1,0:T(8,128)} %bitcast.10, f32[384,1024]{1,0:T(8,128)} %bitcast.11, f32[1536,256]{1,0:T(8,128)} %bitcast.12, f32[1536,256]{1,0:T(8,128)} %bitcast.13, ...), custom_call_target="tpu_custom_call" | custom-call | tf_op jit(solution)/shard_map/acoustic/pallas_call | solution.py:379
  95.5 3.5 %write_out.1 = (f32[384,1024]{1,0:T(8,128)}, f32[384,1024]{1,0:T(8,128)}, f32[1536,256]{1,0:T(8,128)}, f32[1536,256]{1,0:T(8,128)}, f32[1536,256]{1,0:T(8,128)}) custom-call(f32[8,384,128]{2,1,0:T(8,128)S(1)} %get-tuple-element.15.refs_0_, f32[8,384,128]{2,1,0:T(8,128)S(1)} %get-tuple-element.16.refs_1_, f32[2,1536,128]{2,1,0:T(8,128)S(1)} %get-tuple-element.17.refs_2_, ...), custom_call_target="tpu_custom_call" | custom-call | tf_op jit(solution)/shard_map/write_out/pallas_call | solution.py:417
Async XLA Ops:
  0.6 1.1 %copy-start = (f32[4,192,192]{2,1,0:T(8,128)S(1)}, f32[4,192,192]{2,1,0:T(8,128)}, u32[]{:S(2)}) copy-start(f32[4,192,192]{2,1,0:T(8,128)} %inv_hbm.1) | copy-start | bytes 1769476
  1.8 0.7 copy-start.1
